TPU v7x, 512 devices: a whole 4x8x8 slice. The times are simulated.
512 devices in a mesh: pitch: 32 (over x, z), span: 8 (over y), row: 2 (over core).
Axes of the slice: x: 4, y: 8, z: 8, core: 2. Of those that a mesh axis runs over, the one named last changes fastest.
Arguments:
- fields: float32 [3, 512, 128, 512], P(None, 'pitch', 'span', 'row'), may hold values from -6 to 6
- diffusivity: float32 [512, 128, 512], P('pitch', 'span', 'row'), may hold values from 0.01 to 0.1
- mean_flow: bfloat16 [128, 2, 512], P('span', None, 'row'), may hold values from -6 to 6
- radial_kernel: bfloat16 [128, 128], replicated
- tracer_values: float32 [10, 1048576], P(None, ('pitch', 'span', 'row')), may hold values from -6 to 6
- tracer_cells: int32 [1048576], P(('pitch', 'span', 'row')), may hold values from 0 to 65535
- tracer_dest: int32 [1048576, 1], P(('pitch', 'span', 'row')), may hold values from 0 to 31; in each aligned block of 2048 rows (0 to 2047, 2048 to 4095, ...) at most 128 rows name the same one
- interface_map: int32 [2, 512], P('row', 'pitch'), may hold values from 0 to 511, as said below
Outputs:
- advected: float32 [3, 512, 128, 512], P(None, 'pitch', 'span', 'row')
- arrived: float32 [10, 2097152], P(None, ('pitch', 'span', 'row'))
Inputs may be any that keep to these rules, and one draw needn't show every extreme that they name: `tracer_cells`: the local index of the owning cell within the block of the device that holds the tracer, i * 16 * 256 + r * 256 + a for local indices i, r, a. `tracer_dest`: at most 128 of the tracers of one device go to one pitch index. `interface_map`: for one offset o of each draw, row 0 holds (i + o) mod 512 and row 1 holds (i - o) mod 512, so the two rows are inverse permutations.
All inputs are finite; a program needn't handle non-finite values.
Results may differ from a plain program's by a relative error of at most 0.0015.
Values may be sent and summed in bfloat16 or wider, within the bound.
A program may use at most 128 MiB of HBM per device.

v0:
```python
import jax
import jax.numpy as jnp
from jax import lax
from jax.sharding import PartitionSpec as P

SUB = 2
TIME_STEP = 0.9
AXIAL_SPEED = 0.15
PITCH_SPEED = 0.15


def swapped(block, axis, apart):
    count = lax.axis_size(axis)
    route = []
    for low in range(count):
        high = low | 1 << apart
        if high != low and high < count:
            route += [(low, high), (high, low)]
    return lax.ppermute(block, axis, route)


def padded(cells, sides, width):
    for axis, dim in sides:
        count = lax.axis_size(axis)
        head = lax.slice_in_dim(cells, 0, width, axis=dim)
        tail = lax.slice_in_dim(cells, cells.shape[dim] - width, cells.shape[dim], axis=dim)
        cells = jnp.concatenate(
            [
                lax.ppermute(tail, axis, [(i, (i + 1) % count) for i in range(count)]),
                cells,
                lax.ppermute(head, axis, [((i + 1) % count, i) for i in range(count)]),
            ],
            axis=dim,
        )
    return cells


def face_flux(left_values, right_values, left_kappa, right_kappa, face_speed):
    diffusion = -0.5 * (left_kappa + right_kappa) * (right_values - left_values)
    if face_speed is None:
        return diffusion
    return (
        jnp.maximum(face_speed, 0.0) * left_values
        + jnp.minimum(face_speed, 0.0) * right_values
        + diffusion
    )


def interface_ghost(own_face, local_map):
    across = swapped(own_face, "row", 0)
    picked = lax.all_gather(across, "pitch", axis=1, tiled=True)
    return jnp.take(picked, local_map, axis=1)


def update_core(extended, speed_axial, speed_pitch, ghost_face, wall_mask, row_id):
    along_pitch = extended[:, :, 1:-1, :]
    pitch_flux = face_flux(
        along_pitch[:3, :-1],
        along_pitch[:3, 1:],
        along_pitch[3, :-1],
        along_pitch[3, 1:],
        speed_pitch,
    )
    along_radius = extended[:, 1:-1]
    radial_flux = (
        face_flux(
            along_radius[:3, :, :-1],
            along_radius[:3, :, 1:],
            along_radius[3, :, :-1],
            along_radius[3, :, 1:],
            None,
        )
        * wall_mask[:, None]
    )
    core = extended[:, 1:-1, 1:-1]
    pitch_cells = core.shape[1]
    full_stack = jnp.concatenate(
        [core, jnp.broadcast_to(speed_axial[None, None], (1, pitch_cells) + speed_axial.shape)], 0
    )
    upstream = jnp.where(row_id == 0, full_stack[..., 0], ghost_face)
    downstream = jnp.where(row_id == 0, ghost_face, full_stack[..., -1])
    line = jnp.concatenate([upstream[..., None], full_stack, downstream[..., None]], -1)
    face_speed = 0.5 * (line[4, ..., :-1] + line[4, ..., 1:])
    axial_flux = face_flux(
        line[:3, ..., :-1], line[:3, ..., 1:], line[3, ..., :-1], line[3, ..., 1:], face_speed
    )
    divergence = (
        pitch_flux[:, 1:]
        - pitch_flux[:, :-1]
        + radial_flux[:, :, 1:]
        - radial_flux[:, :, :-1]
        + axial_flux[..., 1:]
        - axial_flux[..., :-1]
    )
    return core[:3] - TIME_STEP * divergence


def advance(state, diffusivity, speed_axial, speed_pitch, local_map, wall_mask):
    pitch_cells = state.shape[1]
    stacked = jnp.concatenate([state, diffusivity[None]], 0)
    extended = padded(stacked, (("pitch", 1), ("span", 2)), 1)
    full_stack = jnp.concatenate(
        [stacked, jnp.broadcast_to(speed_axial[None, None], (1, pitch_cells) + speed_axial.shape)],
        0,
    )
    row_id = lax.axis_index("row")
    own_face = jnp.where(row_id == 0, full_stack[..., -1], full_stack[..., 0])
    ghost_face = interface_ghost(own_face, local_map)
    return update_core(extended, speed_axial, speed_pitch, ghost_face, wall_mask, row_id)


def local(
    fields,
    diffusivity,
    mean_flow,
    radial_kernel,
    tracer_values,
    tracer_cells,
    tracer_dest,
    interface_map,
):
    radial_cells = mean_flow.shape[0]
    axial_cells = mean_flow.shape[2]
    flat_width = 2 * axial_cells
    span_id = lax.axis_index("span")
    kernel_cols = lax.dynamic_slice_in_dim(radial_kernel, span_id * radial_cells, radial_cells, 1)
    flat_rows = mean_flow.reshape(radial_cells, flat_width)
    smoothed = lax.psum_scatter(
        jnp.dot(kernel_cols, flat_rows, preferred_element_type=jnp.float32),
        "span",
        scatter_dimension=0,
        tiled=True,
    )
    smoothed = smoothed.reshape(radial_cells, 2, axial_cells)
    speed_axial = AXIAL_SPEED * (1.0 + 0.5 * jnp.tanh(smoothed[:, 0]))
    speed_pitch = PITCH_SPEED * jnp.tanh(smoothed[:, 1])
    plane_size = radial_cells * axial_cells
    sample_fields = jnp.take(fields.reshape(fields.shape[0], -1), tracer_cells, axis=1)
    sample_speed = jnp.take(
        jnp.stack([speed_axial, speed_pitch]).reshape(2, plane_size),
        tracer_cells % plane_size,
        axis=1,
    )
    sampled = jnp.concatenate([sample_fields, sample_speed], 0)
    head_rows = tracer_values[:5]
    tail_rows = tracer_values[5:]
    updated = jnp.concatenate(
        [head_rows + 0.5 * (sampled - head_rows), tail_rows + 0.8 * sampled], 0
    )
    npitch = lax.axis_size("pitch")
    capacity = 2 * tracer_values.shape[1] // npitch
    targets = tracer_dest[:, 0]
    onehot = (targets[:, None] == jnp.arange(npitch, dtype=jnp.int32)[None]).astype(jnp.int32)
    slot_index = jnp.sum((jnp.cumsum(onehot, 0) - onehot) * onehot, 1)
    position = targets * capacity + slot_index
    outgoing = (
        jnp.zeros((tracer_values.shape[0], npitch * capacity), jnp.float32)
        .at[:, position]
        .set(updated)
    )
    arrived = lax.all_to_all(outgoing, "pitch", split_axis=1, concat_axis=1, tiled=True)
    face_index = span_id * radial_cells + jnp.arange(radial_cells + 1, dtype=jnp.int32)
    total_radial = radial_cells * lax.axis_size("span")
    wall_mask = ((face_index > 0) & (face_index < total_radial)).astype(jnp.float32)
    local_map = interface_map[0]
    current = fields
    for substep in range(SUB):
        current = advance(current, diffusivity, speed_axial, speed_pitch, local_map, wall_mask)
    return (current, arrived)


def solution(mesh):
    placed = (
        P(None, "pitch", "span", "row"),
        P("pitch", "span", "row"),
        P("span", None, "row"),
        P(),
        P(None, ("pitch", "span", "row")),
        P(("pitch", "span", "row")),
        P(("pitch", "span", "row"), None),
        P("row", "pitch"),
    )
    return jax.shard_map(
        local,
        mesh=mesh,
        in_specs=placed,
        out_specs=(P(None, "pitch", "span", "row"), P(None, ("pitch", "span", "row"))),
        check_vma=False,
    )
```

profile of v0, /device:TPU:24, one launch (start us, length us, event | category | flops | bytes accessed | tf_op | source)
XLA Modules:
  0.0 287.4 jit_solution(10924218289385498217)
XLA Ops:
  10.5 4.3 %collective-permute-start = (f32[4,1,16,256]{3,2,1,0:T(8,128)}, f32[4,1,16,256]{3,2,1,0:T(8,128)S(1)}, u32[]{:S(2)}, u32[]{:S(2)}) collective-permute-start(f32[4,1,16,256]{3,2,1,0:T(8,128)} %get-tuple-element.57), channel_id=1, source_target_pairs={{0,16},{16,32},{32,48},{48,64},{64,80},{80,96},{96,112},{112,128},... | collective-permute-start | bytes 196616 | tf_op jit(solution)/shard_map/ppermute | solution.py:29
  14.7 10.8 %collective-permute-start.1 = (f32[4,1,16,256]{3,2,1,0:T(8,128)}, f32[4,1,16,256]{3,2,1,0:T(8,128)}, u32[]{:S(2)}, u32[]{:S(2)}) collective-permute-start(f32[4,1,16,256]{3,2,1,0:T(8,128)} %get-tuple-element.58), channel_id=1, source_target_pairs={{16,0},{32,16},{48,32},{64,48},{80,64},{96,80},{112,96},{128,112},... | collective-permute-start | bytes 196616 | tf_op jit(solution)/shard_map/ppermute | solution.py:31
  27.7 16.7 %copy.818 = f32[3,16,16,256]{0,3,2,1:T(8,128)} copy(f32[3,16,16,256]{3,2,1,0:T(8,128)S(1)} %copy-done.2) | data formatting | bytes 1572864 | tf_op args[0]
  44.4 18.2 %gather_fusion = f32[2048,3]{1,0:T(8,128)} fusion(f32[3,65536]{0,1:T(8,128)} %bitcast.121, s32[2048]{0:T(1024)S(1)} %get-tuple-element.74), kind=kCustom, calls=%fused_computation.2 | custom fusion | bytes 57344 | tf_op jit(solution)/shard_map/jit(_take)/gather | solution.py:138
  62.6 2.6 select_bitcast_fusion.1
  65.2 2.2 copy.820
  67.3 9.1 %reduce-window.6 = s32[32,16,128]{2,1,0:T(8,128)S(1)} reduce-window(s32[32,16,128]{2,1,0:T(8,128)S(1)} %fusion.43, s32[]{:T(128)} %constant.30.clone.1), window={size=1x1x128 pad=0_0x0_0x127_0}, to_apply=%region_1.0 | reduce-window | flops 8323072 | bytes 524292 | tf_op jit(solution)/shard_map/reduce-window
  79.0 4.7 %collective-permute-start.2 = (f32[4,18,1,256]{3,0,2,1:T(4,128)S(1)}, f32[4,18,1,256]{3,0,2,1:T(4,128)S(1)}, u32[]{:S(2)}, u32[]{:S(2)}) collective-permute-start(f32[4,18,1,256]{3,0,2,1:T(4,128)S(1)} %copy.846), channel_id=1, source_target_pairs={{0,2},{2,4},{4,6},{6,8},{8,10},{10,12},{12,14},{14,0},{1,3},{3,5},... | collective-permute-start | bytes 221192 | tf_op jit(solution)/shard_map/ppermute | solution.py:29
  85.7 2.2 fusion.14
  98.8 7.6 %gather_fusion.1 = f32[2048,2]{1,0:T(8,128)} fusion(f32[2,4096]{0,1:T(8,128)S(1)} %copy.819, s32[2048]{0:T(1024)S(1)} %get-tuple-element.75), kind=kCustom, calls=%fused_computation.3 | custom fusion | bytes 40960 | tf_op jit(solution)/shard_map/jit(_take)/gather | solution.py:139
  109.8 6.5 %scatter_custom_fusion = f32[10,4096]{0,1:T(8,128)S(1)} fusion(s32[2048]{0:T(1024)} %bitcast.141, f32[2048,10]{1,0:T(8,128)} %copy.822, f32[]{:T(128)} %constant.45.clone.1), kind=kCustom, calls=%fused_computation.51 | custom fusion | bytes 164352 | tf_op jit(solution)/shard_map/scatter | solution.py:159
  117.6 5.2 %all-to-all-start = ((f32[10,32,128]{2,0,1:T(8,128)}), f32[10,32,128]{2,0,1:T(8,128)}, u32[]{:S(2)}, u32[]{:S(2)}) async-start(f32[10,32,128]{2,0,1:T(8,128)} %copy.823), calls=%async_computation.1 | async-start | bytes 524288 | tf_op jit(solution)/shard_map/all_to_all | solution.py:161
  122.8 2.5 fusion.5
  126.2 51.2 %all_gather.6 = f32[5,512,16]{2,1,0:T(8,128)S(1)} all-gather(f32[5,16,16]{2,1,0:T(8,128)S(1)} %copy.782), channel_id=1, replica_groups=mesh['pitch'=32,'span'=8,'row'=2] {'pitch'}, dimensions={1}, use_global_device_ids=true | all-gather | bytes 168960 | tf_op jit(solution)/shard_map/all_gather | solution.py:51
  177.3 2.2 copy.783
  179.5 2.8 gather_fusion.2
  183.9 2.2 copy.786
  198.8 2.7 collective-permute-start.5
  201.4 6.5 %collective-permute-start.6 = (f32[4,1,16,256]{3,2,1,0:T(8,128)S(1)}, f32[4,1,16,256]{3,2,1,0:T(8,128)S(1)}, u32[]{:S(2)}, u32[]{:S(2)}) collective-permute-start(f32[4,1,16,256]{3,2,1,0:T(8,128)S(1)} %get-tuple-element.54), channel_id=1, source_target_pairs={{16,0},{32,16},{48,32},{64,48},{80,64},{96,80},{112,96},{128,112},... | collective-permute-start | bytes 196616 | tf_op jit(solution)/shard_map/ppermute | solution.py:31
  208.0 47.9 %all_gather.7 = f32[5,512,16]{2,1,0:T(8,128)S(1)} all-gather(f32[5,16,16]{2,1,0:T(8,128)S(1)} %copy.807), channel_id=1, replica_groups=mesh['pitch'=32,'span'=8,'row'=2] {'pitch'}, dimensions={1}, use_global_device_ids=true | all-gather | bytes 168960 | tf_op jit(solution)/shard_map/all_gather | solution.py:51
  255.8 2.2 copy.808
  258.0 2.1 gather_fusion.3
  264.8 4.3 %collective-permute-start.7 = (f32[4,18,1,256]{3,0,2,1:T(4,128)S(1)}, f32[4,18,1,256]{3,0,2,1:T(4,128)S(1)}, u32[]{:S(2)}, u32[]{:S(2)}) collective-permute-start(f32[4,18,1,256]{3,0,2,1:T(4,128)S(1)} %copy.851), channel_id=1, source_target_pairs={{0,2},{2,4},{4,6},{6,8},{8,10},{10,12},{12,14},{14,0},{1,3},{3,5},... | collective-permute-start | bytes 221192 | tf_op jit(solution)/shard_map/ppermute | solution.py:29
  273.2 3.3 %collective-permute-done.8 = f32[4,18,1,256]{3,0,2,1:T(4,128)S(1)} collective-permute-done((f32[4,18,1,256]{3,0,2,1:T(4,128)S(1)}, f32[4,18,1,256]{3,0,2,1:T(4,128)S(1)}, u32[]{:S(2)}, u32[]{:S(2)}) %collective-permute-start.8) | collective-permute-done | bytes 73760 | tf_op jit(solution)/shard_map/ppermute | solution.py:31
  (142 shorter events, 52.9 us)
Async XLA Ops:
  7.2 18.4 %copy-start = (bf16[128,128]{1,0:T(8,128)(2,1)S(1)}, bf16[128,128]{1,0:T(8,128)(2,1)}, u32[]{:S(2)}) copy-start(bf16[128,128]{1,0:T(8,128)(2,1)} %param.13) | copy-start | bytes 98308
  7.2 85.3 %reduce-scatter.2.cloned.1.call-start = ((), (), s32[]{:S(2)}) async-start(), calls=%async_computation.2 | async-start | bytes 294912 | tf_op jit(solution)/shard_map/reduce_scatter | solution.py:128
  8.3 17.2 %copy-start.12 = (bf16[16,2,256]{2,1,0:T(2,128)(2,1)S(1)}, bf16[16,2,256]{2,1,0:T(2,128)(2,1)}, u32[]{:S(2)}) copy-start(bf16[16,2,256]{2,1,0:T(2,128)(2,1)} %param.12) | copy-start | bytes 49156
  8.3 18.2 %copy-start.2 = (f32[3,16,16,256]{3,2,1,0:T(8,128)S(1)}, f32[3,16,16,256]{3,2,1,0:T(8,128)}, u32[]{:S(2)}) copy-start(f32[3,16,16,256]{3,2,1,0:T(8,128)} %param.10) | copy-start | bytes 2359300
  9.8 17.2 %copy-start.16 = (s32[1,16]{1,0:T(1,128)S(1)}, s32[1,16]{1,0:T(1,128)}, u32[]{:S(2)}) copy-start(s32[1,16]{1,0:T(1,128)} %param.17) | copy-start | bytes 196
  9.8 17.9 %copy-start.11 = (s32[2048]{0:T(1024)S(1)}, s32[2048]{0:T(1024)}, u32[]{:S(2)}) copy-start(s32[2048]{0:T(1024)} %param.15) | copy-start | bytes 24580
  10.5 67.4 %collective-permute-start = (f32[4,1,16,256]{3,2,1,0:T(8,128)}, f32[4,1,16,256]{3,2,1,0:T(8,128)S(1)}, u32[]{:S(2)}, u32[]{:S(2)}) collective-permute-start(f32[4,1,16,256]{3,2,1,0:T(8,128)} %get-tuple-element.57), channel_id=1, source_target_pairs={{0,16},{16,32},{32,48},{48,64},{64,80},{80,96},{96,112},{112,128},... | collective-permute-start | bytes 196616 | tf_op jit(solution)/shard_map/ppermute | solution.py:29
  14.7 63.1 %collective-permute-start.1 = (f32[4,1,16,256]{3,2,1,0:T(8,128)}, f32[4,1,16,256]{3,2,1,0:T(8,128)}, u32[]{:S(2)}, u32[]{:S(2)}) collective-permute-start(f32[4,1,16,256]{3,2,1,0:T(8,128)} %get-tuple-element.58), channel_id=1, source_target_pairs={{16,0},{32,16},{48,32},{64,48},{80,64},{96,80},{112,96},{128,112},... | collective-permute-start | bytes 196616 | tf_op jit(solution)/shard_map/ppermute | solution.py:31
  27.0 66.3 %copy-start.3 = (f32[3,16,16,256]{3,1,2,0:T(8,128)}, f32[3,16,16,256]{3,1,2,0:T(8,128)S(1)}, u32[]{:S(2)}) copy-start(f32[3,16,16,256]{3,1,2,0:T(8,128)S(1)} %copy.791) | copy-start | bytes 2359300
  62.6 4.7 %copy-start.10 = (s32[2048,1]{0,1:T(1,128)S(1)}, s32[2048,1]{0,1:T(1,128)}, u32[]{:S(2)}) copy-start(s32[2048,1]{0,1:T(1,128)} %param.16) | copy-start | bytes 24580
  77.9 13.4 %copy-start.13 = (f32[17]{0:T(128)}, f32[17]{0:T(128)S(1)}, u32[]{:S(2)}) copy-start(f32[17]{0:T(128)S(1)} %and_convert_fusion) | copy-start | bytes 208
  79.0 10.6 %collective-permute-start.2 = (f32[4,18,1,256]{3,0,2,1:T(4,128)S(1)}, f32[4,18,1,256]{3,0,2,1:T(4,128)S(1)}, u32[]{:S(2)}, u32[]{:S(2)}) collective-permute-start(f32[4,18,1,256]{3,0,2,1:T(4,128)S(1)} %copy.846), channel_id=1, source_target_pairs={{0,2},{2,4},{4,6},{6,8},{8,10},{10,12},{12,14},{14,0},{1,3},{3,5},... | collective-permute-start | bytes 221192 | tf_op jit(solution)/shard_map/ppermute | solution.py:29
  83.7 7.5 %collective-permute-start.3 = (f32[4,18,1,256]{3,0,2,1:T(4,128)S(1)}, f32[4,18,1,256]{3,0,2,1:T(4,128)S(1)}, u32[]{:S(2)}, u32[]{:S(2)}) collective-permute-start(f32[4,18,1,256]{3,0,2,1:T(4,128)S(1)} %copy.847), channel_id=1, source_target_pairs={{2,0},{4,2},{6,4},{8,6},{10,8},{12,10},{14,12},{0,14},{3,1},{5,3},... | collective-permute-start | bytes 221192 | tf_op jit(solution)/shard_map/ppermute | solution.py:31
  96.1 29.2 %collective-permute-start.4 = (f32[5,16,16]{2,0,1:T(8,128)}, f32[5,16,16]{2,0,1:T(8,128)}, u32[]{:S(2)}, u32[]{:S(2)}) collective-permute-start(f32[5,16,16]{2,0,1:T(8,128)} %bitcast_select_fusion.5), channel_id=1, source_target_pairs={{0,1},{1,0},{2,3},{3,2},{4,5},{5,4},{6,7},{7,6},{8,9},{9,8},{10,11... | collective-permute-start | bytes 15368 | tf_op jit(solution)/shard_map/ppermute | solution.py:19
  117.6 161.1 %all-to-all-start = ((f32[10,32,128]{2,0,1:T(8,128)}), f32[10,32,128]{2,0,1:T(8,128)}, u32[]{:S(2)}, u32[]{:S(2)}) async-start(f32[10,32,128]{2,0,1:T(8,128)} %copy.823), calls=%async_computation.1 | async-start | bytes 524288 | tf_op jit(solution)/shard_map/all_to_all | solution.py:161
  177.3 5.0 %copy-start.7 = (f32[5,16,16,1]{2,0,1,3:T(8,128)S(1)}, f32[5,16,16,1]{2,0,1,3:T(8,128)}, u32[]{:S(2)}) copy-start(f32[5,16,16,1]{2,0,1,3:T(8,128)} %copy-done.6) | copy-start | bytes 15364
  177.3 5.0 %copy-start.15 = (pred[16]{0:T(512)(128)(4,1)S(1)}, pred[16]{0:T(512)(128)(4,1)}, u32[]{:S(2)}) copy-start(pred[16]{0:T(512)(128)(4,1)} %compare_and_fusion.2) | copy-start | bytes 52
  179.5 8.0 %copy-start.4 = (f32[3,16,16,256]{3,1,2,0:T(8,128)S(1)}, f32[3,16,16,256]{3,1,2,0:T(8,128)}, u32[]{:S(2)}) copy-start(f32[3,16,16,256]{3,1,2,0:T(8,128)} %copy-done.3) | copy-start | bytes 2359300
  196.2 11.7 %collective-permute-start.9 = (f32[5,16,16]{2,0,1:T(8,128)S(1)}, f32[5,16,16]{2,0,1:T(8,128)S(1)}, u32[]{:S(2)}, u32[]{:S(2)}) collective-permute-start(f32[5,16,16]{2,0,1:T(8,128)S(1)} %bitcast_select_fusion.2), channel_id=1, source_target_pairs={{0,1},{1,0},{2,3},{3,2},{4,5},{5,4},{6,7},{7,6},{8,9},{9,8},{10,11... | collective-permute-start | bytes 15368 | tf_op jit(solution)/shard_map/ppermute | solution.py:19
  198.8 65.5 %collective-permute-start.5 = (f32[4,1,16,256]{3,2,1,0:T(8,128)}, f32[4,1,16,256]{3,2,1,0:T(8,128)S(1)}, u32[]{:S(2)}, u32[]{:S(2)}) collective-permute-start(f32[4,1,16,256]{3,2,1,0:T(8,128)} %get-tuple-element.53), channel_id=1, source_target_pairs={{0,16},{16,32},{32,48},{48,64},{64,80},{80,96},{96,112},{112,128},... | collective-permute-start | bytes 196616 | tf_op jit(solution)/shard_map/ppermute | solution.py:29
  201.4 62.9 %collective-permute-start.6 = (f32[4,1,16,256]{3,2,1,0:T(8,128)S(1)}, f32[4,1,16,256]{3,2,1,0:T(8,128)S(1)}, u32[]{:S(2)}, u32[]{:S(2)}) collective-permute-start(f32[4,1,16,256]{3,2,1,0:T(8,128)S(1)} %get-tuple-element.54), channel_id=1, source_target_pairs={{16,0},{32,16},{48,32},{64,48},{80,64},{96,80},{112,96},{128,112},... | collective-permute-start | bytes 196616 | tf_op jit(solution)/shard_map/ppermute | solution.py:31
  264.8 7.7 %collective-permute-start.7 = (f32[4,18,1,256]{3,0,2,1:T(4,128)S(1)}, f32[4,18,1,256]{3,0,2,1:T(4,128)S(1)}, u32[]{:S(2)}, u32[]{:S(2)}) collective-permute-start(f32[4,18,1,256]{3,0,2,1:T(4,128)S(1)} %copy.851), channel_id=1, source_target_pairs={{0,2},{2,4},{4,6},{6,8},{8,10},{10,12},{12,14},{14,0},{1,3},{3,5},... | collective-permute-start | bytes 221192 | tf_op jit(solution)/shard_map/ppermute | solution.py:29
  269.0 7.5 %collective-permute-start.8 = (f32[4,18,1,256]{3,0,2,1:T(4,128)S(1)}, f32[4,18,1,256]{3,0,2,1:T(4,128)S(1)}, u32[]{:S(2)}, u32[]{:S(2)}) collective-permute-start(f32[4,18,1,256]{3,0,2,1:T(4,128)S(1)} %copy.852), channel_id=1, source_target_pairs={{2,0},{4,2},{6,4},{8,6},{10,8},{12,10},{14,12},{0,14},{3,1},{5,3},... | collective-permute-start | bytes 221192 | tf_op jit(solution)/shard_map/ppermute | solution.py:31
  272.4 4.2 %copy-start.14 = (f32[17]{0:T(128)S(1)}, f32[17]{0:T(128)}, u32[]{:S(2)}) copy-start(f32[17]{0:T(128)} %copy-done.13) | copy-start | bytes 208
  (5 other events, 11.4 us)
Sparse Core Ops, SparseCore 0:
  26.7 35.2 reduce-scatter.1
where the time goes:
time: 289 us; the launch traced here: 287 us
  blocking collectives  99 us (34%)
  local copies, waits for them, and re-layouts  89.4 us (31%)
  starting transfers between devices  46.3 us (16%)
  other arithmetic  32.7 us (11%)
  between operations  14.8 us (5%)
  waiting for transfers between devices  4.27 us (1%)
    all_gather x2, blocking collectives, interface_ghost(): picked = lax.all_gather(across, 'pitch', axis=1, tiled=True)  99 us
    unnamed x53, local copies, waits for them, and re-layouts  24.7 us
    ppermute x4, starting transfers between devices, padded(): lax.ppermute(head, axis, [((i + 1) % count, i) for i in range(count)])  21.3 us
    gather x1, local copies, waits for them, and re-layouts, local(): jnp.take(fields.reshape(fields.shape[0], -1), tracer_cells, axis=1)  18.2 us
    ppermute x4, starting transfers between devices, padded(): lax.ppermute(tail, axis, [(i, (i + 1) % count) for i in range(count)])  15.9 us
    another operation x3, other arithmetic  9.41 us
    gather x1, local copies, waits for them, and re-layouts, local(): jnp.take(jnp.stack([speed_axial, speed_pitch]).reshape(2, plane_size), tr...  7.6 us
    scatter x1, local copies, waits for them, and re-layouts, local(): outgoing = jnp.zeros((tracer_values.shape[0], npitch * capacity), jnp.flo...  6.46 us
  transfers between devices with their start and end apart: 12, of which 2 were waited for; matrix products, arithmetic and copies ran while one was open for 39% of the time, Pallas kernels for 0%

commit v1 on v0

--- a/solution.py
+++ b/solution.py
@@ -48,7 +48,8 @@
 
 def interface_ghost(own_face, local_map):
     across = swapped(own_face, "row", 0)
-    picked = lax.all_gather(across, "pitch", axis=1, tiled=True)
+    copies = jnp.concatenate([across] * lax.axis_size("pitch"), axis=1)
+    picked = lax.all_to_all(copies, "pitch", 1, 1, tiled=True)
     return jnp.take(picked, local_map, axis=1)
 
 

time: 289 us -> 223 us (0.77)
  the two profiles are of different devices: /device:TPU:24 before, /device:TPU:30 now
where the time goes in v1:
time: 223 us; the launch traced here: 221 us
  local copies, waits for them, and re-layouts  94.5 us (42%)
  starting transfers between devices  58.4 us (26%)
  other arithmetic  35.1 us (16%)
  waiting for transfers between devices  17 us (8%)
  between operations  15.4 us (7%)
    unnamed x125, local copies, waits for them, and re-layouts  35.9 us
    gather x1, local copies, waits for them, and re-layouts, local(): jnp.take(fields.reshape(fields.shape[0], -1), tracer_cells, axis=1)  18.2 us
    ppermute x4, starting transfers between devices, padded(): lax.ppermute(head, axis, [((i + 1) % count, i) for i in range(count)])  17.5 us
    ppermute x4, starting transfers between devices, padded(): lax.ppermute(tail, axis, [(i, (i + 1) % count) for i in range(count)])  16.6 us
    all_to_all x2, starting transfers between devices, interface_ghost(): picked = lax.all_to_all(copies, 'pitch', 1, 1, tiled=True)  13.1 us
    all_to_all x1, waiting for transfers between devices, local(): lax.all_to_all(outgoing, 'pitch', split_axis=1, concat_axis=1, tiled=True)  9.6 us
    another operation x3, other arithmetic  9.41 us
    gather x1, local copies, waits for them, and re-layouts, local(): jnp.take(jnp.stack([speed_axial, speed_pitch]).reshape(2, plane_size), tr...  7.6 us
  transfers between devices with their start and end apart: 14, of which 4 were waited for; matrix products, arithmetic and copies ran while one was open for 41% of the time, Pallas kernels for 0%

profile of v1, /device:TPU:30, one launch (start us, length us, event | category | flops | bytes accessed | tf_op | source)
XLA Modules:
  0.0 221.2 jit_solution(11641126282921251363)
XLA Ops:
  10.5 4.3 %collective-permute-start = (f32[4,1,16,256]{3,2,1,0:T(8,128)}, f32[4,1,16,256]{3,2,1,0:T(8,128)S(1)}, u32[]{:S(2)}, u32[]{:S(2)}) collective-permute-start(f32[4,1,16,256]{3,2,1,0:T(8,128)} %get-tuple-element.57), channel_id=1, source_target_pairs={{0,16},{16,32},{32,48},{48,64},{64,80},{80,96},{96,112},{112,128},... | collective-permute-start | bytes 196616 | tf_op jit(solution)/shard_map/ppermute | solution.py:29
  14.7 8.9 %collective-permute-start.1 = (f32[4,1,16,256]{3,2,1,0:T(8,128)}, f32[4,1,16,256]{3,2,1,0:T(8,128)}, u32[]{:S(2)}, u32[]{:S(2)}) collective-permute-start(f32[4,1,16,256]{3,2,1,0:T(8,128)} %get-tuple-element.58), channel_id=1, source_target_pairs={{16,0},{32,16},{48,32},{64,48},{80,64},{96,80},{112,96},{128,112},... | collective-permute-start | bytes 196616 | tf_op jit(solution)/shard_map/ppermute | solution.py:31
  25.7 16.7 %copy.912 = f32[3,16,16,256]{0,3,2,1:T(8,128)} copy(f32[3,16,16,256]{3,2,1,0:T(8,128)S(1)} %copy-done.2) | data formatting | bytes 1572864 | tf_op args[0]
  42.4 18.2 %gather_fusion = f32[2048,3]{1,0:T(8,128)} fusion(f32[3,65536]{0,1:T(8,128)} %bitcast.125, s32[2048]{0:T(1024)S(1)} %get-tuple-element.74), kind=kCustom, calls=%fused_computation.2 | custom fusion | bytes 57344 | tf_op jit(solution)/shard_map/jit(_take)/gather | solution.py:139
  60.6 2.5 %select_bitcast_fusion.1 = f32[3,2048]{0,1:T(8,128)} fusion(f32[2048,3]{1,0:T(8,128)} %gather_fusion, pred[2048]{0:T(1024)(128)(4,1)S(1)} %get-tuple-element.72), kind=kLoop, calls=%fused_computation.50 | loop fusion | flops 6144 | bytes 51200 | tf_op jit(solution)/shard_map/jit(_take)/select_n | solution.py:139
  63.2 2.2 copy.914
  65.4 9.1 %reduce-window.6 = s32[32,16,128]{2,1,0:T(8,128)S(1)} reduce-window(s32[32,16,128]{2,1,0:T(8,128)S(1)} %fusion.43, s32[]{:T(128)} %constant.30.clone.1), window={size=1x1x128 pad=0_0x0_0x127_0}, to_apply=%region_1.0 | reduce-window | flops 8323072 | bytes 524292 | tf_op jit(solution)/shard_map/reduce-window
  77.0 4.7 %collective-permute-start.2 = (f32[4,18,1,256]{3,0,2,1:T(4,128)S(1)}, f32[4,18,1,256]{3,0,2,1:T(4,128)S(1)}, u32[]{:S(2)}, u32[]{:S(2)}) collective-permute-start(f32[4,18,1,256]{3,0,2,1:T(4,128)S(1)} %copy.940), channel_id=1, source_target_pairs={{0,2},{2,4},{4,6},{6,8},{8,10},{10,12},{12,14},{14,0},{1,3},{3,5},... | collective-permute-start | bytes 221192 | tf_op jit(solution)/shard_map/ppermute | solution.py:29
  83.7 2.2 fusion.14
  96.8 7.6 %gather_fusion.1 = f32[2048,2]{1,0:T(8,128)} fusion(f32[2,4096]{0,1:T(8,128)S(1)} %copy.913, s32[2048]{0:T(1024)S(1)} %get-tuple-element.75), kind=kCustom, calls=%fused_computation.3 | custom fusion | bytes 40960 | tf_op jit(solution)/shard_map/jit(_take)/gather | solution.py:140
  107.8 6.5 %scatter_custom_fusion = f32[10,4096]{0,1:T(8,128)S(1)} fusion(s32[2048]{0:T(1024)} %bitcast.149, f32[2048,10]{1,0:T(8,128)} %copy.916, f32[]{:T(128)} %constant.45.clone.1), kind=kCustom, calls=%fused_computation.51 | custom fusion | bytes 164352 | tf_op jit(solution)/shard_map/scatter | solution.py:160
  115.6 7.4 %all-to-all-start.2 = ((f32[10,32,128]{2,0,1:T(8,128)}), f32[10,32,128]{2,0,1:T(8,128)}, u32[]{:S(2)}, u32[]{:S(2)}) async-start(f32[10,32,128]{2,0,1:T(8,128)} %copy.917), calls=%async_computation.3 | async-start | bytes 524288 | tf_op jit(solution)/shard_map/all_to_all | solution.py:162
  124.7 9.6 %all-to-all-done.2 = f32[10,32,128]{2,0,1:T(8,128)} async-done(((f32[10,32,128]{2,0,1:T(8,128)}), f32[10,32,128]{2,0,1:T(8,128)}, u32[]{:S(2)}, u32[]{:S(2)}) %all-to-all-start.2) | async-done | bytes 163872 | tf_op jit(solution)/shard_map/all_to_all | solution.py:162
  134.3 6.2 %all-to-all-start = ((f32[32,1,1280]{2,1,0:T(1,128)}), f32[32,1,1280]{2,1,0:T(1,128)S(1)}, u32[]{:S(2)}, u32[]{:S(2)}) async-start(f32[32,1,1280]{2,1,0:T(1,128)} %reshape.191), calls=%async_computation.1 | async-start | bytes 327680 | tf_op jit(solution)/shard_map/all_to_all | solution.py:52
  140.5 2.5 %fusion.5 = f32[3,17,16,256]{3,1,2,0:T(8,128)S(1)} fusion(f32[3,17,16,256]{3,2,1,0:T(8,128)} %get-tuple-element.56, f32[3,17,16,256]{3,2,1,0:T(8,128)} %get-tuple-element.55, f32[17,16,256]{2,0,1:T(8,128)} %copy.867, f32[16,256]{1,0:T(8,128)S(1)} %get-tuple-element.70, f32[16,256]{1,0:T(8,128)S(1)} %get-tuple-element.71), kind=kLoop, calls=%fused_computation.32 | loop fusion | flops 1253376 | bytes 2818048 | tf_op jit(solution)/shard_map/add | solution.py:43
  145.0 4.1 %all-to-all-done = f32[32,1,1280]{2,1,0:T(1,128)S(1)} async-done(((f32[32,1,1280]{2,1,0:T(1,128)}), f32[32,1,1280]{2,1,0:T(1,128)S(1)}, u32[]{:S(2)}, u32[]{:S(2)}) %all-to-all-start) | async-done | bytes 163872 | tf_op jit(solution)/shard_map/all_to_all | solution.py:52
  152.7 2.8 %gather_fusion.2 = f32[16,5,16]{2,1,0:T(8,128)} fusion(f32[5,512,16]{2,0,1:T(8,128)} %bitcast.136, s32[1024]{0:T(1024)S(1)} %pad_clamp_fusion), kind=kCustom, calls=%fused_computation.clone | custom fusion | bytes 10304 | tf_op jit(solution)/shard_map/jit(_take)/gather | solution.py:53
  169.9 3.4 %collective-permute-start.5 = (f32[4,1,16,256]{3,2,1,0:T(8,128)S(1)}, f32[4,1,16,256]{3,2,1,0:T(8,128)S(1)}, u32[]{:S(2)}, u32[]{:S(2)}) collective-permute-start(f32[4,1,16,256]{3,2,1,0:T(8,128)S(1)} %get-tuple-element.53), channel_id=1, source_target_pairs={{0,16},{16,32},{32,48},{48,64},{64,80},{80,96},{96,112},{112,128},... | collective-permute-start | bytes 196616 | tf_op jit(solution)/shard_map/ppermute | solution.py:29
  173.3 4.6 %collective-permute-start.6 = (f32[4,1,16,256]{3,2,1,0:T(8,128)S(1)}, f32[4,1,16,256]{3,2,1,0:T(8,128)S(1)}, u32[]{:S(2)}, u32[]{:S(2)}) collective-permute-start(f32[4,1,16,256]{3,2,1,0:T(8,128)S(1)} %get-tuple-element.54), channel_id=1, source_target_pairs={{16,0},{32,16},{48,32},{64,48},{80,64},{96,80},{112,96},{128,112},... | collective-permute-start | bytes 196616 | tf_op jit(solution)/shard_map/ppermute | solution.py:31
  179.7 2.9 %reshape.193 = f32[32,1,1280]{2,1,0:T(1,128)} reshape(f32[512,5,16]{2,1,0:T(8,128)} %bitcast.134) | data formatting | bytes 327680
  182.6 6.9 %all-to-all-start.1 = ((f32[32,1,1280]{2,1,0:T(1,128)}), f32[32,1,1280]{2,1,0:T(1,128)S(1)}, u32[]{:S(2)}, u32[]{:S(2)}) async-start(f32[32,1,1280]{2,1,0:T(1,128)} %reshape.193), calls=%async_computation.2 | async-start | bytes 327680 | tf_op jit(solution)/shard_map/all_to_all | solution.py:52
  190.0 4.2 %collective-permute-start.7 = (f32[4,18,1,256]{3,0,2,1:T(4,128)S(1)}, f32[4,18,1,256]{3,0,2,1:T(4,128)S(1)}, u32[]{:S(2)}, u32[]{:S(2)}) collective-permute-start(f32[4,18,1,256]{3,0,2,1:T(4,128)S(1)} %copy.945), channel_id=1, source_target_pairs={{0,2},{2,4},{4,6},{6,8},{8,10},{10,12},{12,14},{14,0},{1,3},{3,5},... | collective-permute-start | bytes 221192 | tf_op jit(solution)/shard_map/ppermute | solution.py:29
  199.4 2.3 %collective-permute-done.8 = f32[4,18,1,256]{3,0,2,1:T(4,128)S(1)} collective-permute-done((f32[4,18,1,256]{3,0,2,1:T(4,128)S(1)}, f32[4,18,1,256]{3,0,2,1:T(4,128)S(1)}, u32[]{:S(2)}, u32[]{:S(2)}) %collective-permute-start.8) | collective-permute-done | bytes 73760 | tf_op jit(solution)/shard_map/ppermute | solution.py:31
  205.2 2.1 gather_fusion.3
  (217 shorter events, 64.1 us)
Async XLA Ops:
  7.2 16.5 %copy-start = (bf16[128,128]{1,0:T(8,128)(2,1)S(1)}, bf16[128,128]{1,0:T(8,128)(2,1)}, u32[]{:S(2)}) copy-start(bf16[128,128]{1,0:T(8,128)(2,1)} %param.13) | copy-start | bytes 98308
  7.2 17.4 %copy-start.2 = (f32[3,16,16,256]{3,2,1,0:T(8,128)S(1)}, f32[3,16,16,256]{3,2,1,0:T(8,128)}, u32[]{:S(2)}) copy-start(f32[3,16,16,256]{3,2,1,0:T(8,128)} %param.10) | copy-start | bytes 2359300
  7.2 16.4 %copy-start.15 = (bf16[16,2,256]{2,1,0:T(2,128)(2,1)S(1)}, bf16[16,2,256]{2,1,0:T(2,128)(2,1)}, u32[]{:S(2)}) copy-start(bf16[16,2,256]{2,1,0:T(2,128)(2,1)} %param.12) | copy-start | bytes 49156
  7.2 83.3 %reduce-scatter.2.cloned.1.call-start = ((), (), s32[]{:S(2)}) async-start(), calls=%async_computation.4 | async-start | bytes 294912 | tf_op jit(solution)/shard_map/reduce_scatter | solution.py:129
  8.4 16.7 %copy-start.19 = (s32[1,16]{1,0:T(1,128)S(1)}, s32[1,16]{1,0:T(1,128)}, u32[]{:S(2)}) copy-start(s32[1,16]{1,0:T(1,128)} %param.17) | copy-start | bytes 196
  8.4 17.2 %copy-start.14 = (s32[2048]{0:T(1024)S(1)}, s32[2048]{0:T(1024)}, u32[]{:S(2)}) copy-start(s32[2048]{0:T(1024)} %param.15) | copy-start | bytes 24580
  10.5 65.5 %collective-permute-start = (f32[4,1,16,256]{3,2,1,0:T(8,128)}, f32[4,1,16,256]{3,2,1,0:T(8,128)S(1)}, u32[]{:S(2)}, u32[]{:S(2)}) collective-permute-start(f32[4,1,16,256]{3,2,1,0:T(8,128)} %get-tuple-element.57), channel_id=1, source_target_pairs={{0,16},{16,32},{32,48},{48,64},{64,80},{80,96},{96,112},{112,128},... | collective-permute-start | bytes 196616 | tf_op jit(solution)/shard_map/ppermute | solution.py:29
  14.7 61.2 %collective-permute-start.1 = (f32[4,1,16,256]{3,2,1,0:T(8,128)}, f32[4,1,16,256]{3,2,1,0:T(8,128)}, u32[]{:S(2)}, u32[]{:S(2)}) collective-permute-start(f32[4,1,16,256]{3,2,1,0:T(8,128)} %get-tuple-element.58), channel_id=1, source_target_pairs={{16,0},{32,16},{48,32},{64,48},{80,64},{96,80},{112,96},{128,112},... | collective-permute-start | bytes 196616 | tf_op jit(solution)/shard_map/ppermute | solution.py:31
  25.1 66.3 %copy-start.3 = (f32[3,16,16,256]{3,1,2,0:T(8,128)}, f32[3,16,16,256]{3,1,2,0:T(8,128)S(1)}, u32[]{:S(2)}) copy-start(f32[3,16,16,256]{3,1,2,0:T(8,128)S(1)} %copy.887) | copy-start | bytes 2359300
  42.4 22.9 %copy-start.13 = (s32[2048,1]{0,1:T(1,128)S(1)}, s32[2048,1]{0,1:T(1,128)}, u32[]{:S(2)}) copy-start(s32[2048,1]{0,1:T(1,128)} %param.16) | copy-start | bytes 24580
  75.9 13.4 %copy-start.17 = (f32[17]{0:T(128)}, f32[17]{0:T(128)S(1)}, u32[]{:S(2)}) copy-start(f32[17]{0:T(128)S(1)} %and_convert_fusion) | copy-start | bytes 208
  77.0 10.5 %collective-permute-start.2 = (f32[4,18,1,256]{3,0,2,1:T(4,128)S(1)}, f32[4,18,1,256]{3,0,2,1:T(4,128)S(1)}, u32[]{:S(2)}, u32[]{:S(2)}) collective-permute-start(f32[4,18,1,256]{3,0,2,1:T(4,128)S(1)} %copy.940), channel_id=1, source_target_pairs={{0,2},{2,4},{4,6},{6,8},{8,10},{10,12},{12,14},{14,0},{1,3},{3,5},... | collective-permute-start | bytes 221192 | tf_op jit(solution)/shard_map/ppermute | solution.py:29
  81.7 7.5 %collective-permute-start.3 = (f32[4,18,1,256]{3,0,2,1:T(4,128)S(1)}, f32[4,18,1,256]{3,0,2,1:T(4,128)S(1)}, u32[]{:S(2)}, u32[]{:S(2)}) collective-permute-start(f32[4,18,1,256]{3,0,2,1:T(4,128)S(1)} %copy.941), channel_id=1, source_target_pairs={{2,0},{4,2},{6,4},{8,6},{10,8},{12,10},{14,12},{0,14},{3,1},{5,3},... | collective-permute-start | bytes 221192 | tf_op jit(solution)/shard_map/ppermute | solution.py:31
  94.1 28.9 %collective-permute-start.4 = (f32[5,16,16]{2,0,1:T(8,128)}, f32[5,16,16]{2,0,1:T(8,128)S(1)}, u32[]{:S(2)}, u32[]{:S(2)}) collective-permute-start(f32[5,16,16]{2,0,1:T(8,128)} %bitcast_select_fusion.5), channel_id=1, source_target_pairs={{0,1},{1,0},{2,3},{3,2},{4,5},{5,4},{6,7},{7,6},{8,9},{9,8},{10,11... | collective-permute-start | bytes 15368 | tf_op jit(solution)/shard_map/ppermute | solution.py:19
  115.6 18.8 %all-to-all-start.2 = ((f32[10,32,128]{2,0,1:T(8,128)}), f32[10,32,128]{2,0,1:T(8,128)}, u32[]{:S(2)}, u32[]{:S(2)}) async-start(f32[10,32,128]{2,0,1:T(8,128)} %copy.917), calls=%async_computation.3 | async-start | bytes 524288 | tf_op jit(solution)/shard_map/all_to_all | solution.py:162
  134.3 14.7 %all-to-all-start = ((f32[32,1,1280]{2,1,0:T(1,128)}), f32[32,1,1280]{2,1,0:T(1,128)S(1)}, u32[]{:S(2)}, u32[]{:S(2)}) async-start(f32[32,1,1280]{2,1,0:T(1,128)} %reshape.191), calls=%async_computation.1 | async-start | bytes 327680 | tf_op jit(solution)/shard_map/all_to_all | solution.py:52
  143.0 12.4 %copy-start.9 = (f32[5,16,16,1]{2,0,1,3:T(8,128)S(1)}, f32[5,16,16,1]{2,0,1,3:T(8,128)}, u32[]{:S(2)}) copy-start(f32[5,16,16,1]{2,0,1,3:T(8,128)} %copy-done.8) | copy-start | bytes 15364
  143.0 12.4 %copy-start.16 = (pred[16]{0:T(512)(128)(4,1)S(1)}, pred[16]{0:T(512)(128)(4,1)}, u32[]{:S(2)}) copy-start(pred[16]{0:T(512)(128)(4,1)} %compare_and_fusion.2) | copy-start | bytes 52
  167.9 9.9 %collective-permute-start.9 = (f32[5,16,16]{2,0,1:T(8,128)S(1)}, f32[5,16,16]{2,0,1:T(8,128)S(1)}, u32[]{:S(2)}, u32[]{:S(2)}) collective-permute-start(f32[5,16,16]{2,0,1:T(8,128)S(1)} %bitcast_select_fusion.2), channel_id=1, source_target_pairs={{0,1},{1,0},{2,3},{3,2},{4,5},{5,4},{6,7},{7,6},{8,9},{9,8},{10,11... | collective-permute-start | bytes 15368 | tf_op jit(solution)/shard_map/ppermute | solution.py:19
  169.9 19.7 %collective-permute-start.5 = (f32[4,1,16,256]{3,2,1,0:T(8,128)S(1)}, f32[4,1,16,256]{3,2,1,0:T(8,128)S(1)}, u32[]{:S(2)}, u32[]{:S(2)}) collective-permute-start(f32[4,1,16,256]{3,2,1,0:T(8,128)S(1)} %get-tuple-element.53), channel_id=1, source_target_pairs={{0,16},{16,32},{32,48},{48,64},{64,80},{80,96},{96,112},{112,128},... | collective-permute-start | bytes 196616 | tf_op jit(solution)/shard_map/ppermute | solution.py:29
  173.3 16.3 %collective-permute-start.6 = (f32[4,1,16,256]{3,2,1,0:T(8,128)S(1)}, f32[4,1,16,256]{3,2,1,0:T(8,128)S(1)}, u32[]{:S(2)}, u32[]{:S(2)}) collective-permute-start(f32[4,1,16,256]{3,2,1,0:T(8,128)S(1)} %get-tuple-element.54), channel_id=1, source_target_pairs={{16,0},{32,16},{48,32},{64,48},{80,64},{96,80},{112,96},{128,112},... | collective-permute-start | bytes 196616 | tf_op jit(solution)/shard_map/ppermute | solution.py:31
  182.6 19.5 %all-to-all-start.1 = ((f32[32,1,1280]{2,1,0:T(1,128)}), f32[32,1,1280]{2,1,0:T(1,128)S(1)}, u32[]{:S(2)}, u32[]{:S(2)}) async-start(f32[32,1,1280]{2,1,0:T(1,128)} %reshape.193), calls=%async_computation.2 | async-start | bytes 327680 | tf_op jit(solution)/shard_map/all_to_all | solution.py:52
  190.0 8.7 %collective-permute-start.7 = (f32[4,18,1,256]{3,0,2,1:T(4,128)S(1)}, f32[4,18,1,256]{3,0,2,1:T(4,128)S(1)}, u32[]{:S(2)}, u32[]{:S(2)}) collective-permute-start(f32[4,18,1,256]{3,0,2,1:T(4,128)S(1)} %copy.945), channel_id=1, source_target_pairs={{0,2},{2,4},{4,6},{6,8},{8,10},{10,12},{12,14},{14,0},{1,3},{3,5},... | collective-permute-start | bytes 221192 | tf_op jit(solution)/shard_map/ppermute | solution.py:29
  194.3 7.5 %collective-permute-start.8 = (f32[4,18,1,256]{3,0,2,1:T(4,128)S(1)}, f32[4,18,1,256]{3,0,2,1:T(4,128)S(1)}, u32[]{:S(2)}, u32[]{:S(2)}) collective-permute-start(f32[4,18,1,256]{3,0,2,1:T(4,128)S(1)} %copy.946), channel_id=1, source_target_pairs={{2,0},{4,2},{6,4},{8,6},{10,8},{12,10},{14,12},{0,14},{3,1},{5,3},... | collective-permute-start | bytes 221192 | tf_op jit(solution)/shard_map/ppermute | solution.py:31
  (10 other events, 35.0 us)
Sparse Core Ops, SparseCore 0:
  24.7 37.1 reduce-scatter.1
